TPU v7x, 512 devices: a whole 4x8x8 slice. The times are simulated.
512 devices in a mesh: slab: 64 (over z, y), mode: 8 (over x, core).
Axes of the slice: x: 4, y: 8, z: 8, core: 2. Of those that a mesh axis runs over, the one named last changes fastest.
Arguments:
- block_input: float32 [64, 512, 2048], P('mode', 'slab'), may hold values from -6 to 6
- drum_mask: int32 [512, 2048], P('slab'), may hold values 0 or 1
- panel: float32 [64, 512, 2048], P('mode', 'slab'), may hold values from -120 to 120, as said below
Outputs:
- filtered: float32 [64, 512, 2048], P('mode', 'slab')
- orthonormal: float32 [64, 512, 2048], P('mode', 'slab')
Inputs may be any that keep to these rules, and one draw needn't show every extreme that they name: The panel's entries.
All inputs are finite; a program needn't handle non-finite values. No bound on the sum of `drum_mask` on one device may be relied on, other than what follows from the above.
Results may differ from a plain program's by a relative error of at most 0.000096.
Values sent between devices are 32-bit elements; how exact they have to be, the bound alone decides.
A program may use at most 64 MiB of HBM per device.

v0:
```python
import jax
import jax.numpy as jnp
from jax import lax
from jax.sharding import PartitionSpec as P

DEGREE = 8


center_point = 5.0
half_width = 3.0
floor_estimate = 0.0


def with_halo(block, sides, width):
    for axis, dim in sides:
        count = lax.axis_size(axis)
        forward = [(i, i + 1) for i in range(count - 1)]
        backward = [(target, source) for source, target in forward]
        low = lax.ppermute(
            lax.slice_in_dim(block, block.shape[dim] - width, None, axis=dim), axis, forward
        )
        high = lax.ppermute(lax.slice_in_dim(block, 0, width, axis=dim), axis, backward)
        block = jnp.concatenate([low, block, high], axis=dim)
    return block


def filter_coefficients():
    sigma_first = half_width / (floor_estimate - center_point)
    result = [(sigma_first / half_width, 0.0)]
    sigma_now = sigma_first
    for step in range(DEGREE - 1):
        sigma_next = 1.0 / (2.0 / sigma_first - sigma_now)
        result.append((2.0 * sigma_next / half_width, sigma_now * sigma_next))
        sigma_now = sigma_next
    return result


def chol_solve(factor, rhs):
    inner = lax.linalg.triangular_solve(factor, rhs, left_side=True, lower=True)
    return lax.linalg.triangular_solve(factor, inner, left_side=True, lower=True, transpose_a=True)


def stencil(extended, mask_part):
    middle = extended[:, 1:-1]
    col_padded = jnp.pad(middle, ((0, 0), (0, 0), (1, 1)))
    beside = extended[:, 2:] + extended[:, :-2] + col_padded[:, :, 2:] + col_padded[:, :, :-2]
    return mask_part * (4.0 * middle - beside)


def single_filter(started, mask_float):
    current = started
    previous = started
    for scale_img, scale_old in filter_coefficients():
        extended = with_halo(current, (("slab", 1),), 1)
        applied = stencil(extended, mask_float)
        newest = scale_img * (applied - center_point * current)
        if scale_old != 0.0:
            newest = newest - scale_old * previous
        previous, current = (current, newest)
    return current


def shards(block_input, drum_mask, panel):
    highest = lax.Precision.HIGHEST
    mask_float = drum_mask.astype(jnp.float32)
    started = block_input * mask_float
    filtered = single_filter(started, mask_float)
    own_width = filtered.shape[0]
    mode_index = lax.axis_index("mode")
    gathered = lax.all_gather(filtered, "mode", axis=0, tiled=True)
    panel_full = lax.all_gather(panel, "mode", axis=0, tiled=True)
    block_all = gathered.shape[0]
    total_cells = lax.axis_size("slab") * gathered.shape[1] * gathered.shape[2]
    filtered_mat = gathered.reshape(block_all, -1)
    panel_mat = panel_full.reshape(block_all, -1)
    local_zz = jnp.dot(filtered_mat, filtered_mat.T, precision=highest)
    local_cross = jnp.dot(filtered_mat, panel_mat.T, precision=highest)
    gram_zz, cross_gram = lax.psum((local_zz, local_cross), "slab")
    factor_zz = jnp.linalg.cholesky(gram_zz)
    project = chol_solve(factor_zz, cross_gram)
    panel_new = panel_mat - jnp.dot(project.T, filtered_mat, precision=highest)
    local_new = jnp.dot(panel_new, panel_new.T, precision=highest)
    gram_new = lax.psum(local_new, "slab") / total_cells
    lower_part = jnp.linalg.cholesky(gram_new)
    inverse = lax.linalg.triangular_solve(
        lower_part, jnp.eye(block_all, dtype=jnp.float32), left_side=True, lower=True
    )
    row_block = lax.dynamic_slice_in_dim(inverse, mode_index * own_width, own_width, 0)
    mixed = jnp.dot(row_block, project.T, precision=highest)
    orthonormal = jnp.dot(row_block, panel_mat, precision=highest) - jnp.dot(
        mixed, filtered_mat, precision=highest
    )
    return (filtered, orthonormal.reshape(filtered.shape))


def solution(mesh):
    placed = (P("mode", "slab", None), P("slab", None), P("mode", "slab", None))
    return jax.shard_map(
        shards,
        mesh=mesh,
        in_specs=placed,
        out_specs=(P("mode", "slab", None), P("mode", "slab", None)),
        check_vma=False,
    )
```

profile of v0, /device:TPU:2, one launch (start us, length us, event | category | flops | bytes accessed | tf_op | source)
XLA Modules:
  0.0 760.3 jit_solution(8452050957069636062)
XLA Ops:
  10.8 4.5 collective-permute-start.1
  15.6 1.6 collective-permute-done.1
  18.9 4.9 collective-permute-start.3
  24.1 1.6 collective-permute-done.3
  27.6 4.9 collective-permute-start.5
  32.8 1.6 collective-permute-done.5
  36.1 4.9 collective-permute-start.7
  41.3 1.6 collective-permute-done.7
  44.5 5.0 collective-permute-start.9
  49.8 1.6 collective-permute-done.9
  53.1 6.1 collective-permute-start.11
  59.5 1.6 collective-permute-done.11
  62.8 6.1 collective-permute-start.13
  69.2 1.6 collective-permute-done.13
  72.4 6.3 collective-permute-start.15
  78.9 1.6 collective-permute-done.15
  81.6 2.1 copy.27
  83.8 6.6 copy.33
  90.4 52.8 %all-gather.5.cloned.1.call-done = f32[64,8,2048]{2,0,1:T(8,128)} async-done(((f32[8,8,2048]{2,0,1:T(8,128)}), f32[64,8,2048]{2,0,1:T(8,128)}) %all-gather.5.cloned.1.call-update) | async-done | bytes 4194320 | tf_op jit(solution)/shard_map/all_gather | solution.py:70
  143.2 9.1 %fusion.2 = f32[64,64]{1,0:T(8,128)S(1)} fusion(f32[64,8,2048]{2,0,1:T(8,128)} %all-gather.5.cloned.1.call-done, f32[64,8,2048]{2,1,0:T(8,128)} %all-gather.3.cloned.1.call-done), kind=kOutput, calls=%fused_computation.4 | convolution fusion | flops 805306368 | bytes 8404992 | tf_op jit(solution)/shard_map/dot_general | solution.py:77
  152.4 3.6 convolution_bitcast_fusion
  156.0 280.2 %all-reduce.8 = (f32[64,64]{1,0:T(8,128)S(1)}, f32[64,64]{0,1:T(8,128)S(1)}) all-reduce(f32[64,64]{1,0:T(8,128)S(1)} %fusion.2, f32[64,64]{0,1:T(8,128)S(1)} %convolution_bitcast_fusion), channel_id=1, replica_groups=mesh['slab'=64,'mode'=8] {'slab'}, use_global_device_ids=true, to_apply=%region_3.5 | all-reduce | flops 8192 | bytes 65536 | tf_op jit(solution)/shard_map/psum | solution.py:78
  436.3 5.8 cholesky.44
  443.5 4.9 custom-call.8
  448.8 2.6 copy.32
  452.2 3.7 convolution_subtract_fusion
  456.0 3.4 fusion.96
  459.4 274.2 %psum.23 = f32[64,64]{0,1:T(8,128)S(1)} all-reduce(f32[64,64]{0,1:T(8,128)S(1)} %fusion.96), channel_id=1, replica_groups=mesh['slab'=64,'mode'=8] {'slab'}, use_global_device_ids=true, to_apply=%region_4.7 | all-reduce | flops 4096 | bytes 32768 | tf_op jit(solution)/shard_map/psum | solution.py:83
  733.7 5.8 cholesky.55
  740.9 4.9 custom-call.11
  746.2 4.0 fusion.83
  750.3 2.1 convolution_subtract_fusion.1
  (65 shorter events, 24.4 us)
Async XLA Ops:
  7.2 18.5 %copy-start.4 = (f32[8,8,2048]{2,1,0:T(8,128)S(1)}, f32[8,8,2048]{2,1,0:T(8,128)}, u32[]{:S(2)}) copy-start(f32[8,8,2048]{2,1,0:T(8,128)} %param.6) | copy-start | bytes 1572868
  7.2 76.6 %all-gather.3.cloned.1.call-start = ((), (), s32[]{:S(2)}) async-start(), calls=%async_computation | async-start | bytes 4718592 | tf_op jit(solution)/shard_map/all_gather | solution.py:71
  9.5 6.2 collective-permute-start
  10.8 6.4 collective-permute-start.1
  15.4 127.9 %all-gather.5.cloned.1.call-start = ((), (), s32[]{:S(2)}) async-start(), calls=%async_computation.1 | async-start | bytes 4718592 | tf_op jit(solution)/shard_map/all_gather | solution.py:70
  17.6 6.5 collective-permute-start.2
  18.9 6.8 collective-permute-start.3
  26.3 6.5 collective-permute-start.4
  27.6 6.8 collective-permute-start.5
  34.8 6.5 collective-permute-start.6
  36.1 6.8 collective-permute-start.7
  43.2 6.6 collective-permute-start.8
  44.5 6.9 collective-permute-start.9
  51.8 7.7 %collective-permute-start.10 = (f32[8,1,2048]{2,0,1:T(8,128)S(1)}, f32[8,1,2048]{2,0,1:T(8,128)S(1)}, u32[]{:S(2)}, u32[]{:S(2)}) collective-permute-start(f32[8,1,2048]{2,0,1:T(8,128)S(1)} %get-tuple-element.18), channel_id=1, source_target_pairs={{8,0},{16,8},{24,16},{32,24},{40,32},{48,40},{56,48},{64,56},{72,6... | collective-permute-start | bytes 196616 | tf_op jit(solution)/shard_map/ppermute | solution.py:22
  53.1 8.0 %collective-permute-start.11 = (f32[8,1,2048]{2,0,1:T(8,128)S(1)}, f32[8,1,2048]{2,0,1:T(8,128)S(1)}, u32[]{:S(2)}, u32[]{:S(2)}) collective-permute-start(f32[8,1,2048]{2,0,1:T(8,128)S(1)} %get-tuple-element.19), channel_id=1, source_target_pairs={{0,8},{8,16},{16,24},{24,32},{32,40},{40,48},{48,56},{56,64},{64,7... | collective-permute-start | bytes 196616 | tf_op jit(solution)/shard_map/ppermute | solution.py:19
  61.5 7.7 %collective-permute-start.12 = (f32[8,1,2048]{2,0,1:T(8,128)S(1)}, f32[8,1,2048]{2,0,1:T(8,128)S(1)}, u32[]{:S(2)}, u32[]{:S(2)}) collective-permute-start(f32[8,1,2048]{2,0,1:T(8,128)S(1)} %get-tuple-element.16), channel_id=1, source_target_pairs={{8,0},{16,8},{24,16},{32,24},{40,32},{48,40},{56,48},{64,56},{72,6... | collective-permute-start | bytes 196616 | tf_op jit(solution)/shard_map/ppermute | solution.py:22
  62.8 8.0 %collective-permute-start.13 = (f32[8,1,2048]{2,0,1:T(8,128)S(1)}, f32[8,1,2048]{2,0,1:T(8,128)S(1)}, u32[]{:S(2)}, u32[]{:S(2)}) collective-permute-start(f32[8,1,2048]{2,0,1:T(8,128)S(1)} %get-tuple-element.17), channel_id=1, source_target_pairs={{0,8},{8,16},{16,24},{24,32},{32,40},{40,48},{48,56},{56,64},{64,7... | collective-permute-start | bytes 196616 | tf_op jit(solution)/shard_map/ppermute | solution.py:19
  71.1 7.7 %collective-permute-start.14 = (f32[8,1,2048]{2,0,1:T(8,128)S(1)}, f32[8,1,2048]{2,0,1:T(8,128)S(1)}, u32[]{:S(2)}, u32[]{:S(2)}) collective-permute-start(f32[8,1,2048]{2,0,1:T(8,128)S(1)} %get-tuple-element.14), channel_id=1, source_target_pairs={{8,0},{16,8},{24,16},{32,24},{40,32},{48,40},{56,48},{64,56},{72,6... | collective-permute-start | bytes 196616 | tf_op jit(solution)/shard_map/ppermute | solution.py:22
  72.4 8.0 %collective-permute-start.15 = (f32[8,1,2048]{2,0,1:T(8,128)S(1)}, f32[8,1,2048]{2,0,1:T(8,128)S(1)}, u32[]{:S(2)}, u32[]{:S(2)}) collective-permute-start(f32[8,1,2048]{2,0,1:T(8,128)S(1)} %get-tuple-element.15), channel_id=1, source_target_pairs={{0,8},{8,16},{16,24},{24,32},{32,40},{40,48},{48,56},{56,64},{64,7... | collective-permute-start | bytes 196616 | tf_op jit(solution)/shard_map/ppermute | solution.py:19
  143.2 9.1 %copy-start = (f32[64,8,2048]{2,0,1:T(8,128)S(1)}, f32[64,8,2048]{2,0,1:T(8,128)}, u32[]{:S(2)}) copy-start(f32[64,8,2048]{2,0,1:T(8,128)} %all-gather.5.cloned.1.call-done) | copy-start | bytes 12582916
  448.8 3.5 copy-start.1
  451.4 4.6 copy-start.2
  745.8 4.5 copy-start.3
Sparse Core Ops, SparseCore 0:
  15.5 40.9 all-gather.2
  81.7 61.4 all-gather.4
where the time goes:
time: 761 us; the launch traced here: 760 us
  blocking collectives  554 us (73%)
  waiting for transfers between devices  67.7 us (9%)
  starting transfers between devices  53.1 us (7%)
  other arithmetic  30.3 us (4%)
  matrix products  26.8 us (4%)
  between operations  14.5 us (2%)
  local copies, waits for them, and re-layouts  13.6 us (2%)
    psum x1, blocking collectives, shards(): gram_zz, cross_gram = lax.psum((local_zz, local_cross), 'slab')  280 us
    psum x1, blocking collectives, shards(): gram_new = lax.psum(local_new, 'slab') / total_cells  274 us
    all_gather x1, waiting for transfers between devices, shards(): gathered = lax.all_gather(filtered, 'mode', axis=0, tiled=True)  52.8 us
    ppermute x8, starting transfers between devices, with_halo(): lax.ppermute(lax.slice_in_dim(block, block.shape[dim] - width, None, axis...  42.7 us
  transfers between devices with their start and end apart: 18, of which 17 were waited for; matrix products, arithmetic and copies ran while one was open for 2% of the time, Pallas kernels for 0%

commit v1 on v0

v1 whole, which is shorter than its diff:
```python
import functools

import jax
import jax.numpy as jnp
from jax import lax
from jax.experimental import pallas as pl
from jax.experimental.pallas import tpu as pltpu
from jax.sharding import PartitionSpec as P

DEGREE = 8
ROWS_Y = 8
PAD = 128

center_point = 5.0
half_width = 3.0
floor_estimate = 0.0
HIGHEST = lax.Precision.HIGHEST


def filter_coefficients():
    sigma_first = half_width / (floor_estimate - center_point)
    result = [(sigma_first / half_width, 0.0)]
    sigma_now = sigma_first
    for step in range(DEGREE - 1):
        sigma_next = 1.0 / (2.0 / sigma_first - sigma_now)
        result.append((2.0 * sigma_next / half_width, sigma_now * sigma_next))
        sigma_now = sigma_next
    return result


def at(slab, mode):
    return {"slab": slab, "mode": mode}


def remote(src, dst, send, recv, where):
    return pltpu.make_async_remote_copy(
        src_ref=src,
        dst_ref=dst,
        send_sem=send,
        recv_sem=recv,
        device_id=where,
        device_id_type=pl.DeviceIdType.MESH,
    )


def exchange(src, dst, send, recv, count, me, place):
    copies = []
    for j in range(1, count):
        peer = lax.rem(me + j, count)
        copy = remote(
            src(peer), dst(me), send.at[peer], recv.at[me], place(peer)
        )
        copy.start()
        copies.append(copy)
    return copies


def arrive(src, dst, send, recv, count, me, place):
    for j in range(1, count):
        peer = lax.rem(me + j, count)
        remote(src(peer), dst(peer), send.at[peer], recv.at[peer], place(peer)).wait_recv()


def gather_kernel(
    nz, ny, nm, coef_ref, block_ref, mask_ref, panel_ref,
    filt_ref, x_ref, g_ref,
    raw, halo, mraw, mhalo, pt, y, mf, part, rs, tmp, yb, tmpz, zb, tmpg,
    loc_sem, halo_s, halo_r, mask_s, mask_r, p_s, p_r, z_s, z_r, rs_s, rs_r, y_s, y_r, zz_s, zz_r, ag_s, ag_r, out_sem,
):
    ns = nz * ny
    slab = lax.axis_index("slab")
    m = lax.axis_index("mode")
    zi = slab // ny
    yi = lax.rem(slab, ny)
    mb, rows, cols = block_ref.shape
    wide = cols // nm
    up = lax.rem(slab + ns - 1, ns)
    down = lax.rem(slab + 1, ns)

    local = [pltpu.make_async_copy(mask_ref, mraw, loc_sem.at[2 * rows])]
    local += [pltpu.make_async_copy(block_ref.at[:, r, :], raw.at[r], loc_sem.at[r]) for r in range(rows)]
    local += [pltpu.make_async_copy(panel_ref.at[:, r, :], pt.at[r], loc_sem.at[rows + r]) for r in range(rows)]
    for copy in local:
        copy.start()

    barrier = pltpu.get_barrier_semaphore()

    def greet(where):
        pl.semaphore_signal(barrier, inc=1, device_id=where, device_id_type=pl.DeviceIdType.MESH)

    greet(at(up, m))
    greet(at(down, m))
    for j in range(1, nm):
        greet(at(slab, lax.rem(m + j, nm)))
    for j in range(1, ny):
        greet(at(zi * ny + lax.rem(yi + j, ny), m))
    for j in range(1, nz):
        greet(at(lax.rem(zi + j, nz) * ny + yi, m))
    for copy in local[: 1 + rows]:
        copy.wait()
    pl.semaphore_wait(barrier, 2 + nm - 1 + ny - 1 + nz - 1)

    sends = []
    to_down = remote(mraw, mhalo.at[0], mask_s.at[0], mask_r.at[0], at(down, m))
    to_up = remote(mraw, mhalo.at[1], mask_s.at[1], mask_r.at[1], at(up, m))
    mask_copies = [to_down, to_up]
    for copy in mask_copies:
        copy.start()
    halo_copies = [[], []]
    for d in range(1, rows + 1):
        lo, hi = rows - d, d - 1
        top = remote(raw.at[lo], halo.at[0, lo], halo_s.at[0, lo], halo_r.at[0, lo], at(down, m))
        bottom = remote(raw.at[hi], halo.at[1, hi], halo_s.at[1, hi], halo_r.at[1, hi], at(up, m))
        top.start()
        bottom.start()
        halo_copies[0].append(top)
        halo_copies[1].append(bottom)
    for copy in local[1 + rows:]:
        copy.wait()

    def mates(peer):
        return at(slab, peer)

    def along_y(peer):
        return at(zi * ny + peer, m)

    def along_z(peer):
        return at(peer * ny + yi, m)

    def columns(peer):
        return pl.ds(pl.multiple_of(peer * wide, wide), wide)

    def eight(peer, base=0):
        return pl.ds(pl.multiple_of(base + peer * mb, mb), mb)

    nmodes = nm * mb
    p_src = lambda peer: pt.at[:, :, columns(peer)]
    p_dst = lambda who: x_ref.at[:, eight(who, nmodes), :]
    sends += exchange(p_src, p_dst, p_s, p_r, nm, m, mates)
    x_ref[:, eight(m, nmodes), :] = pt[:, :, columns(m)]

    zero_pad = jnp.zeros((mb, PAD), jnp.float32)
    for r in range(rows):
        row = jnp.broadcast_to(mraw[r:r + 1, :].astype(jnp.float32), (mb, cols))
        mf[rows + r, :, :cols] = row
        mf[rows + r, :, cols:] = zero_pad
        y[0, rows + r, :, :cols] = raw[r] * row
        y[0, rows + r, :, cols:] = zero_pad

    def row_step(k, r):
        here = y[k - 1, r]
        total = here + y[k - 1, r - 1] + y[k - 1, r + 1]
        total = total + pltpu.roll(here, 1, 1) + pltpu.roll(here, cols + PAD - 1, 1)
        before = y[jnp.maximum(k - 2, 0), r]
        y[k, r] = mf[r] * (total * coef_ref[0, k]) - before * coef_ref[1, k]

    def stage(d):

        def body(k, carry):
            row_step(k, rows - d + k)
            row_step(k, 2 * rows - 1 + d - k)
            return carry

        lax.fori_loop(1, min(DEGREE, d + 3) + 1, body, 0)

    def inner(k, carry):
        def one(r, c):
            row_step(k, r)
            return c

        return lax.fori_loop(rows + k, 2 * rows - k, one, carry)

    lax.fori_loop(1, rows // 2, inner, 0)

    for copy in mask_copies:
        copy.wait_recv()
    inside = [jnp.where(slab > 0, 1.0, 0.0), jnp.where(slab < ns - 1, 1.0, 0.0)]
    for side in range(2):
        for r in range(rows):
            index = r if side == 0 else 2 * rows + r
            row = mhalo[side, r:r + 1, :].astype(jnp.float32) * inside[side]
            mf[index, :, :cols] = jnp.broadcast_to(row, (mb, cols))
            mf[index, :, cols:] = zero_pad

    z_src = lambda r: (lambda peer: y.at[DEGREE, rows + r, :, columns(peer)])
    z_dst = lambda r: (lambda who: x_ref.at[r, eight(who), :])
    done_rows = []
    for d in range(1, rows + 1):
        for side, r in ((0, rows - d), (1, d - 1)):
            halo_copies[side][d - 1].wait_recv()
            index = r if side == 0 else 2 * rows + r
            y[0, index, :, :cols] = halo[side, r] * mf[index, :, :cols]
            y[0, index, :, cols:] = zero_pad
        stage(d)
        if d > rows // 2:
            for r in (rows - d, d - 1):
                sends += exchange(z_src(r), z_dst(r), z_s.at[r], z_r.at[r], nm, m, mates)
                x_ref[r, eight(m), :] = y[DEGREE, rows + r, :, columns(m)]
                done_rows.append(r)

    outs = [
        pltpu.make_async_copy(y.at[DEGREE, rows + r, :, pl.ds(0, cols)], filt_ref.at[r], out_sem.at[r])
        for r in range(rows)
    ]
    for copy in outs:
        copy.start()

    def reduce_out(which):
        rs[which, m] = part[which, m]
        return exchange(
            lambda peer: part.at[which, peer], lambda who: rs.at[which, who],
            rs_s.at[which], rs_r.at[which], nm, m, mates,
        )

    def sum_and_send(which, from_buf, from_s, from_r, count, me, place, out, to_buf, to_s, to_r, to_count, to_me, to_place):
        arrive(lambda peer: out.at[which], lambda who: from_buf.at[which, who], from_s.at[which], from_r.at[which], count, me, place)
        total = from_buf[which, 0]
        for j in range(1, count):
            total = total + from_buf[which, j]
        out[which] = total
        to_buf[which, to_me] = total
        return exchange(
            lambda peer: out.at[which], lambda who: to_buf.at[which, who],
            to_s.at[which], to_r.at[which], to_count, to_me, to_place,
        )

    def to_y(which):
        return sum_and_send(which, rs, rs_s, rs_r, nm, m, mates, tmp, yb, y_s, y_r, ny, yi, along_y)

    def to_z(which):
        return sum_and_send(which, yb, y_s, y_r, ny, yi, along_y, tmpz, zb, zz_s, zz_r, nz, zi, along_z)

    def to_all(which):
        return sum_and_send(which, zb, zz_s, zz_r, nz, zi, along_z, tmpg, g_ref, ag_s, ag_r, nm, m, mates)

    def finish(which):
        arrive(lambda peer: tmpg.at[which], lambda who: g_ref.at[which, who], ag_s.at[which], ag_r.at[which], nm, m, mates)

    contract = (((1,), (1,)), ((), ()))
    arrive(p_src, p_dst, p_s, p_r, nm, m, mates)
    panel_part = jnp.zeros((nmodes, nmodes), jnp.float32)
    for r in range(rows):
        b = x_ref[r, nmodes:, :]
        panel_part += lax.dot_general(b, b, contract, precision=HIGHEST, preferred_element_type=jnp.float32)
    panel_part = jnp.concatenate([panel_part, jnp.zeros((nmodes, nmodes), jnp.float32)], axis=1)
    for j in range(nm):
        part[1, j] = panel_part[j * mb:(j + 1) * mb]
    sends += reduce_out(1)

    block_part = jnp.zeros((nmodes, 2 * nmodes), jnp.float32)
    for r in done_rows:
        arrive(z_src(r), z_dst(r), z_s.at[r], z_r.at[r], nm, m, mates)
        both = x_ref[r]
        block_part += lax.dot_general(
            both[:nmodes], both, contract, precision=HIGHEST, preferred_element_type=jnp.float32
        )
    for j in range(nm):
        part[0, j] = block_part[j * mb:(j + 1) * mb]
    sends += reduce_out(0)
    sends += to_y(1)
    sends += to_y(0)
    sends += to_z(1)
    sends += to_z(0)
    sends += to_all(1)
    sends += to_all(0)
    finish(1)
    finish(0)

    for copy in outs:
        copy.wait()
    for copy in sends + mask_copies + halo_copies[0] + halo_copies[1]:
        copy.wait_send()


def factor_kernel(n, mb, cells, g_ref, filt_ref, w_ref, out_ref, sem):
    rows = filt_ref.shape[0]
    outs = [pltpu.make_async_copy(filt_ref.at[r], out_ref.at[:, r, :], sem.at[r]) for r in range(rows)]
    for copy in outs:
        copy.start()
    nb = 2 * n // mb
    zeros = jnp.zeros((n, n), jnp.float32)
    top = g_ref[0].reshape(n, 2 * n)
    panel = g_ref[1].reshape(n, 2 * n)
    cross = top[:, n:]
    full = jnp.concatenate(
        [top, jnp.concatenate([cross.T, panel[:, :n]], axis=1)], axis=0
    )
    w_ref[...] = eliminate(full, n, mb, nb, cells)
    for copy in outs:
        copy.wait()


def eliminate(full, n, mb, nb, cells):
    width = 2 * n
    a = [full[i * mb:(i + 1) * mb] for i in range(nb)]
    lane = lax.broadcasted_iota(jnp.int32, (mb, width), 1)
    sub = lax.broadcasted_iota(jnp.int32, (mb, width), 0)
    result = []
    for b in range(nb):
        base = b * mb
        inside = (lane >= base) & (lane < base + mb)
        block = a[b]
        rowb = [jnp.broadcast_to(block[i:i + 1, :], (mb, width)) for i in range(mb)]
        e = [[jnp.broadcast_to(rowb[i][:, base + j:base + j + 1], (mb, width)) for j in range(i + 1)] for i in range(mb)]
        later = range(b + 1, nb)
        column = {
            i: [jnp.broadcast_to(a[i][:, base + k:base + k + 1], (mb, width)) for k in range(mb)] for i in later
        }
        row = [jnp.where(inside, jnp.where(lane == base + i, 1.0, 0.0), rowb[i]) for i in range(mb)]
        pivot, inverse = [], []
        f = [[None] * mb for _ in range(mb)]
        for k in range(mb):
            pivot.append(e[k][k])
            inverse.append(1.0 / e[k][k])
            for i in range(k + 1, mb):
                f[i][k] = e[i][k] * inverse[k]
            for i in range(k + 1, mb):
                for j in range(k + 1, i + 1):
                    e[i][j] = e[i][j] - f[i][k] * e[j][k]
                row[i] = row[i] - f[i][k] * row[k]
        if base >= n:
            scaled = jnp.zeros((mb, width), jnp.float32)
            for i in range(mb):
                scaled = jnp.where(sub == i, row[i] * lax.rsqrt(pivot[i] * (1.0 / cells)), scaled)
            result.append(jnp.where(lane < base + mb, scaled, 0.0))
        if b == nb - 1:
            break
        v = [row[i] * inverse[i] for i in range(mb)]
        for k in reversed(range(mb)):
            for i in range(k):
                v[i] = v[i] - f[k][i] * v[k]
        for i in later:
            total = column[i][0] * v[0]
            for k in range(1, mb):
                total = total + column[i][k] * v[k]
            a[i] = jnp.where(inside, 0.0, a[i]) - total
    return jnp.concatenate(result, axis=0)


def apply_kernel(nm, x_ref, w_ref, out_ref, mixed, send, recv):
    slab = lax.axis_index("slab")
    m = lax.axis_index("mode")
    rows, mb, cols = out_ref.shape
    wide = cols // nm
    barrier = pltpu.get_barrier_semaphore()
    for j in range(1, nm):
        pl.semaphore_signal(
            barrier, inc=1, device_id=at(slab, lax.rem(m + j, nm)), device_id_type=pl.DeviceIdType.MESH
        )
    pl.semaphore_wait(barrier, nm - 1)

    def columns(peer):
        return pl.ds(pl.multiple_of(peer * wide, wide), wide)

    def eight(peer):
        return pl.ds(pl.multiple_of(peer * mb, mb), mb)

    def mates(peer):
        return at(slab, peer)

    src = lambda r: (lambda peer: mixed.at[r, eight(peer), :])
    dst = lambda r: (lambda who: out_ref.at[r, :, columns(who)])
    w = w_ref[...]
    sends = []
    for r in range(rows):
        mixed[r] = jnp.dot(w, x_ref[r], precision=HIGHEST, preferred_element_type=jnp.float32)
        sends += exchange(src(r), dst(r), send.at[r], recv.at[r], nm, m, mates)
        out_ref[r, :, columns(m)] = mixed[r, eight(m), :]
    for r in range(rows):
        arrive(src(r), dst(r), send.at[r], recv.at[r], nm, m, mates)
    for copy in sends:
        copy.wait_send()


def shards(ns, nm, block_input, drum_mask, panel):
    ny = ROWS_Y if ns % ROWS_Y == 0 else 2
    nz = ns // ny
    mb, rows, cols = block_input.shape
    wide = cols // nm
    n = nm * mb
    f32 = jnp.float32
    pairs = filter_coefficients()
    coef = jnp.array(
        [[0.0] + [-first for first, _ in pairs], [0.0] + [second for _, second in pairs]], f32
    )
    vmem = pl.BlockSpec(memory_space=pltpu.VMEM)
    hbm = pl.BlockSpec(memory_space=pl.ANY)
    dma = pltpu.SemaphoreType.DMA
    filt, x, g = pl.pallas_call(
        functools.partial(gather_kernel, nz, ny, nm),
        out_shape=(
            jax.ShapeDtypeStruct((rows, mb, cols), f32),
            jax.ShapeDtypeStruct((rows, 2 * n, wide), f32),
            jax.ShapeDtypeStruct((2, nm, mb, 2 * n), f32),
        ),
        in_specs=[pl.BlockSpec(memory_space=pltpu.SMEM), hbm, hbm, hbm],
        out_specs=(hbm, vmem, vmem),
        scratch_shapes=[
            pltpu.VMEM((rows, mb, cols), f32),
            pltpu.VMEM((2, rows, mb, cols), f32),
            pltpu.VMEM((rows, cols), jnp.int32),
            pltpu.VMEM((2, rows, cols), jnp.int32),
            pltpu.VMEM((rows, mb, cols), f32),
            pltpu.VMEM((DEGREE + 1, 3 * rows, mb, cols + PAD), f32),
            pltpu.VMEM((3 * rows, mb, cols + PAD), f32),
            pltpu.VMEM((2, nm, mb, 2 * n), f32),
            pltpu.VMEM((2, nm, mb, 2 * n), f32),
            pltpu.VMEM((2, mb, 2 * n), f32),
            pltpu.VMEM((2, ny, mb, 2 * n), f32),
            pltpu.VMEM((2, mb, 2 * n), f32),
            pltpu.VMEM((2, nz, mb, 2 * n), f32),
            pltpu.VMEM((2, mb, 2 * n), f32),
            dma((2 * rows + 1,)),
            dma((2, rows)), dma((2, rows)),
            dma((2,)), dma((2,)),
            dma((nm,)), dma((nm,)),
            dma((rows, nm)), dma((rows, nm)),
            dma((2, nm)), dma((2, nm)),
            dma((2, ny)), dma((2, ny)),
            dma((2, nz)), dma((2, nz)),
            dma((2, nm)), dma((2, nm)),
            dma((rows,)),
        ],
        compiler_params=pltpu.CompilerParams(collective_id=0, has_side_effects=True),
        name="filter_gram",
    )(coef, block_input, drum_mask, panel)
    w, filtered = pl.pallas_call(
        functools.partial(factor_kernel, n, mb, float(ns * rows * cols)),
        out_shape=(
            jax.ShapeDtypeStruct((n, 2 * n), f32),
            jax.ShapeDtypeStruct((mb, rows, cols), f32),
        ),
        in_specs=[vmem, hbm],
        out_specs=(vmem, hbm),
        scratch_shapes=[dma((rows,))],
        name="factor",
    )(g, filt)
    spread = pl.pallas_call(
        functools.partial(apply_kernel, nm),
        out_shape=jax.ShapeDtypeStruct((rows, mb, cols), f32),
        in_specs=[vmem, vmem],
        out_specs=vmem,
        scratch_shapes=[
            pltpu.VMEM((rows, n, wide), f32),
            dma((rows, nm)), dma((rows, nm)),
        ],
        compiler_params=pltpu.CompilerParams(collective_id=1, has_side_effects=True),
        name="apply",
    )(x, w)
    return (filtered, jnp.transpose(spread, (1, 0, 2)))


def solution(mesh):
    placed = (P("mode", "slab", None), P("slab", None), P("mode", "slab", None))
    return jax.shard_map(
        functools.partial(shards, mesh.shape["slab"], mesh.shape["mode"]),
        mesh=mesh,
        in_specs=placed,
        out_specs=(P("mode", "slab", None), P("mode", "slab", None)),
        check_vma=False,
    )
```

time: 761 us -> 94.7 us (0.12)
  the two profiles are of different devices: /device:TPU:2 before, /device:TPU:1 now
where the time goes in v1:
time: 94.7 us; the launch traced here: 94.4 us
  Pallas kernels  91.6 us (97%)
  local copies, waits for them, and re-layouts  2.14 us (2%)
    pallas_call x1, Pallas kernels, shards(): pl.pallas_call(functools.partial(gather_kernel, nz, ny, nm), out_shape=(j...  58.9 us
    pallas_call x1, Pallas kernels, shards(): pl.pallas_call(functools.partial(factor_kernel, n, mb, float(ns * rows *...  18.5 us
    pallas_call x1, Pallas kernels, shards(): pl.pallas_call(functools.partial(apply_kernel, nm), out_shape=jax.ShapeDt...  14.2 us
    unnamed x1, local copies, waits for them, and re-layouts  2.14 us

profile of v1, /device:TPU:1, one launch (start us, length us, event | category | flops | bytes accessed | tf_op | source)
XLA Modules:
  0.0 94.4 jit_solution(223067213180075175)
XLA Ops:
  0.6 58.9 %filter_gram.1 = (f32[8,8,2048]{2,1,0:T(8,128)}, f32[8,128,256]{2,1,0:T(8,128)}, f32[2,8,8,128]{3,2,1,0:T(8,128)}) custom-call(f32[2,9]{1,0:T(2,128)} %constant.2.clone.coef_ref, f32[8,8,2048]{2,1,0:T(8,128)} %block_ref.1, s32[8,2048]{1,0:T(8,128)} %mask_ref.1, f32[8,8,2048]{2,1,0:T(8,128)} %panel_ref.1), custom_call_target="tpu_custom_call" | custom-call | tf_op jit(solution)/shard_map/filter_gram/pallas_call | solution.py:389
  59.5 18.5 %factor.1 = (f32[64,128]{1,0:T(8,128)}, f32[8,8,2048]{2,1,0:T(8,128)}) custom-call(f32[2,8,8,128]{3,2,1,0:T(8,128)} %get-tuple-element.7.g_ref, f32[8,8,2048]{2,1,0:T(8,128)} %get-tuple-element.8.filt_ref), custom_call_target="tpu_custom_call" | custom-call | tf_op jit(solution)/shard_map/factor/pallas_call | solution.py:427
  78.0 14.2 %apply.1 = f32[8,8,2048]{2,1,0:T(8,128)} custom-call(f32[8,128,256]{2,1,0:T(8,128)} %get-tuple-element.10.x_ref, f32[64,128]{1,0:T(8,128)} %get-tuple-element.11.w_ref), custom_call_target="tpu_custom_call" | custom-call | tf_op jit(solution)/shard_map/apply/pallas_call | solution.py:438
  92.2 2.1 %copy.6 = f32[8,8,2048]{2,1,0:T(8,128)} copy(f32[8,8,2048]{2,0,1:T(8,128)} %bitcast.1) | data formatting | bytes 1048576

commit v2 on v1

--- a/solution.py
+++ b/solution.py
@@ -10,11 +10,11 @@
 DEGREE = 8
 ROWS_Y = 8
 PAD = 128
+VMEM_LIMIT = 54000 << 10
 
 center_point = 5.0
 half_width = 3.0
 floor_estimate = 0.0
-HIGHEST = lax.Precision.HIGHEST
 
 
 def filter_coefficients():
@@ -61,11 +61,24 @@
         remote(src(peer), dst(peer), send.at[peer], recv.at[peer], place(peer)).wait_recv()
 
 
-def gather_kernel(
-    nz, ny, nm, coef_ref, block_ref, mask_ref, panel_ref,
-    filt_ref, x_ref, g_ref,
-    raw, halo, mraw, mhalo, pt, y, mf, part, rs, tmp, yb, tmpz, zb, tmpg,
-    loc_sem, halo_s, halo_r, mask_s, mask_r, p_s, p_r, z_s, z_r, rs_s, rs_r, y_s, y_r, zz_s, zz_r, ag_s, ag_r, out_sem,
+def pick(k, values):
+    out = jnp.float32(values[0])
+    for index in range(1, len(values)):
+        out = jnp.where(k == index, jnp.float32(values[index]), out)
+    return out
+
+
+def halves(value):
+    high = value.astype(jnp.bfloat16)
+    return high, (value - high.astype(jnp.float32)).astype(jnp.bfloat16)
+
+
+def whole_kernel(
+    nz, ny, nm, cells, block_ref, mask_ref, panel_ref,
+    filt_ref, spread_ref,
+    raw, halo, mraw, mhalo, pt, y, mf, x, xs, part, rs, tmp, yb, tmpz, zb, tmpg, g, mixed,
+    loc_sem, halo_s, halo_r, mask_s, mask_r, p_s, p_r, z_s, z_r, rs_s, rs_r, y_s, y_r, zz_s, zz_r, ag_s, ag_r,
+    back_s, back_r, out_sem,
 ):
     ns = nz * ny
     slab = lax.axis_index("slab")
@@ -74,8 +87,12 @@
     yi = lax.rem(slab, ny)
     mb, rows, cols = block_ref.shape
     wide = cols // nm
+    n = nm * mb
     up = lax.rem(slab + ns - 1, ns)
     down = lax.rem(slab + 1, ns)
+    pairs = filter_coefficients()
+    gain = [0.0] + [-first for first, _ in pairs]
+    drag = [0.0] + [second for _, second in pairs]
 
     local = [pltpu.make_async_copy(mask_ref, mraw, loc_sem.at[2 * rows])]
     local += [pltpu.make_async_copy(block_ref.at[:, r, :], raw.at[r], loc_sem.at[r]) for r in range(rows)]
@@ -101,9 +118,10 @@
     pl.semaphore_wait(barrier, 2 + nm - 1 + ny - 1 + nz - 1)
 
     sends = []
-    to_down = remote(mraw, mhalo.at[0], mask_s.at[0], mask_r.at[0], at(down, m))
-    to_up = remote(mraw, mhalo.at[1], mask_s.at[1], mask_r.at[1], at(up, m))
-    mask_copies = [to_down, to_up]
+    mask_copies = [
+        remote(mraw, mhalo.at[0], mask_s.at[0], mask_r.at[0], at(down, m)),
+        remote(mraw, mhalo.at[1], mask_s.at[1], mask_r.at[1], at(up, m)),
+    ]
     for copy in mask_copies:
         copy.start()
     halo_copies = [[], []]
@@ -133,11 +151,10 @@
     def eight(peer, base=0):
         return pl.ds(pl.multiple_of(base + peer * mb, mb), mb)
 
-    nmodes = nm * mb
     p_src = lambda peer: pt.at[:, :, columns(peer)]
-    p_dst = lambda who: x_ref.at[:, eight(who, nmodes), :]
+    p_dst = lambda who: x.at[:, eight(who, n), :]
     sends += exchange(p_src, p_dst, p_s, p_r, nm, m, mates)
-    x_ref[:, eight(m, nmodes), :] = pt[:, :, columns(m)]
+    x[:, eight(m, n), :] = pt[:, :, columns(m)]
 
     zero_pad = jnp.zeros((mb, PAD), jnp.float32)
     for r in range(rows):
@@ -152,10 +169,9 @@
         total = here + y[k - 1, r - 1] + y[k - 1, r + 1]
         total = total + pltpu.roll(here, 1, 1) + pltpu.roll(here, cols + PAD - 1, 1)
         before = y[jnp.maximum(k - 2, 0), r]
-        y[k, r] = mf[r] * (total * coef_ref[0, k]) - before * coef_ref[1, k]
+        y[k, r] = mf[r] * (total * pick(k, gain)) - before * pick(k, drag)
 
     def stage(d):
-
         def body(k, carry):
             row_step(k, rows - d + k)
             row_step(k, 2 * rows - 1 + d - k)
@@ -183,8 +199,45 @@
             mf[index, :, cols:] = zero_pad
 
     z_src = lambda r: (lambda peer: y.at[DEGREE, rows + r, :, columns(peer)])
-    z_dst = lambda r: (lambda who: x_ref.at[r, eight(who), :])
-    done_rows = []
+    z_dst = lambda r: (lambda who: x.at[r, eight(who), :])
+    contract = (((1,), (1,)), ((), ()))
+
+    def products(left, right):
+        return lax.dot_general(left, right, contract, preferred_element_type=jnp.float32)
+
+    def panel_gram(r):
+        high, low = halves(x[r, n:, :])
+        xs[r, n:2 * n, :] = high
+        xs[r, 3 * n:, :] = low
+        mixed_part = products(high, low)
+        return products(high, high) + products(low, low), mixed_part
+
+    def block_gram(r):
+        arrive(z_src(r), z_dst(r), z_s.at[r], z_r.at[r], nm, m, mates)
+        high, low = halves(x[r, :n, :])
+        xs[r, :n, :] = high
+        xs[r, 2 * n:3 * n, :] = low
+        all_high, all_low = xs[r, :2 * n, :], xs[r, 2 * n:, :]
+        return (
+            products(high, all_high) + products(low, all_low) + products(high, all_low) + products(low, all_high)
+        )
+
+    def reduce_out(which):
+        rs[which, m] = part[which, m]
+        return exchange(
+            lambda peer: part.at[which, peer], lambda who: rs.at[which, who],
+            rs_s.at[which], rs_r.at[which], nm, m, mates,
+        )
+
+    panel_part = jnp.zeros((n, n), jnp.float32)
+    panel_mixed = jnp.zeros((n, n), jnp.float32)
+    block_part = jnp.zeros((n, 2 * n), jnp.float32)
+    quarter = rows // 4
+    panel_rows = {
+        rows - 3: list(range(quarter, rows - quarter)),
+        rows - 2: list(range(quarter)) + list(range(rows - quarter, rows)),
+    }
+    outs = []
     for d in range(1, rows + 1):
         for side, r in ((0, rows - d), (1, d - 1)):
             halo_copies[side][d - 1].wait_recv()
@@ -195,22 +248,26 @@
         if d > rows // 2:
             for r in (rows - d, d - 1):
                 sends += exchange(z_src(r), z_dst(r), z_s.at[r], z_r.at[r], nm, m, mates)
-                x_ref[r, eight(m), :] = y[DEGREE, rows + r, :, columns(m)]
-                done_rows.append(r)
-
-    outs = [
-        pltpu.make_async_copy(y.at[DEGREE, rows + r, :, pl.ds(0, cols)], filt_ref.at[r], out_sem.at[r])
-        for r in range(rows)
-    ]
-    for copy in outs:
-        copy.start()
-
-    def reduce_out(which):
-        rs[which, m] = part[which, m]
-        return exchange(
-            lambda peer: part.at[which, peer], lambda who: rs.at[which, who],
-            rs_s.at[which], rs_r.at[which], nm, m, mates,
-        )
+                x[r, eight(m), :] = y[DEGREE, rows + r, :, columns(m)]
+                out = pltpu.make_async_copy(y.at[DEGREE, rows + r, :, pl.ds(0, cols)], filt_ref.at[r], out_sem.at[r])
+                out.start()
+                outs.append(out)
+        if d in panel_rows:
+            if d == rows - 3:
+                arrive(p_src, p_dst, p_s, p_r, nm, m, mates)
+            for r in panel_rows[d]:
+                same, cross = panel_gram(r)
+                panel_part += same
+                panel_mixed += cross
+        if d == rows - 2:
+            panel_all = panel_part + panel_mixed + panel_mixed.T
+            panel_all = jnp.concatenate([panel_all, jnp.zeros((n, n), jnp.float32)], axis=1)
+            for j in range(nm):
+                part[1, j] = panel_all[j * mb:(j + 1) * mb]
+            sends += reduce_out(1)
+        if d > rows // 2 + 1:
+            for r in (rows - d + 1, d - 2):
+                block_part += block_gram(r)
 
     def sum_and_send(which, from_buf, from_s, from_r, count, me, place, out, to_buf, to_s, to_r, to_count, to_me, to_place):
         arrive(lambda peer: out.at[which], lambda who: from_buf.at[which, who], from_s.at[which], from_r.at[which], count, me, place)
@@ -231,29 +288,13 @@
         return sum_and_send(which, yb, y_s, y_r, ny, yi, along_y, tmpz, zb, zz_s, zz_r, nz, zi, along_z)
 
     def to_all(which):
-        return sum_and_send(which, zb, zz_s, zz_r, nz, zi, along_z, tmpg, g_ref, ag_s, ag_r, nm, m, mates)
+        return sum_and_send(which, zb, zz_s, zz_r, nz, zi, along_z, tmpg, g, ag_s, ag_r, nm, m, mates)
 
     def finish(which):
-        arrive(lambda peer: tmpg.at[which], lambda who: g_ref.at[which, who], ag_s.at[which], ag_r.at[which], nm, m, mates)
-
-    contract = (((1,), (1,)), ((), ()))
-    arrive(p_src, p_dst, p_s, p_r, nm, m, mates)
-    panel_part = jnp.zeros((nmodes, nmodes), jnp.float32)
-    for r in range(rows):
-        b = x_ref[r, nmodes:, :]
-        panel_part += lax.dot_general(b, b, contract, precision=HIGHEST, preferred_element_type=jnp.float32)
-    panel_part = jnp.concatenate([panel_part, jnp.zeros((nmodes, nmodes), jnp.float32)], axis=1)
-    for j in range(nm):
-        part[1, j] = panel_part[j * mb:(j + 1) * mb]
-    sends += reduce_out(1)
-
-    block_part = jnp.zeros((nmodes, 2 * nmodes), jnp.float32)
-    for r in done_rows:
-        arrive(z_src(r), z_dst(r), z_s.at[r], z_r.at[r], nm, m, mates)
-        both = x_ref[r]
-        block_part += lax.dot_general(
-            both[:nmodes], both, contract, precision=HIGHEST, preferred_element_type=jnp.float32
-        )
+        arrive(lambda peer: tmpg.at[which], lambda who: g.at[which, who], ag_s.at[which], ag_r.at[which], nm, m, mates)
+
+    for r in (0, rows - 1):
+        block_part += block_gram(r)
     for j in range(nm):
         part[0, j] = block_part[j * mb:(j + 1) * mb]
     sends += reduce_out(0)
@@ -266,28 +307,30 @@
     finish(1)
     finish(0)
 
+    top = g[0].reshape(n, 2 * n)
+    panel = g[1].reshape(n, 2 * n)
+    full = jnp.concatenate(
+        [top, jnp.concatenate([top[:, n:].T, panel[:, :n]], axis=1)], axis=0
+    )
+    w_high, w_low = halves(eliminate(full, n, mb, 2 * n // mb, cells))
+    back_src = lambda r: (lambda peer: mixed.at[r, eight(peer), :])
+    back_dst = lambda r: (lambda who: spread_ref.at[r, :, columns(who)])
+    for r in range(rows):
+        high, low = xs[r, :2 * n, :], xs[r, 2 * n:, :]
+        mixed[r] = (
+            jnp.dot(w_high, high, preferred_element_type=jnp.float32)
+            + jnp.dot(w_high, low, preferred_element_type=jnp.float32)
+            + jnp.dot(w_low, high, preferred_element_type=jnp.float32)
+        )
+        sends += exchange(back_src(r), back_dst(r), back_s.at[r], back_r.at[r], nm, m, mates)
+        spread_ref[r, :, columns(m)] = mixed[r, eight(m), :]
+    for r in range(rows):
+        arrive(back_src(r), back_dst(r), back_s.at[r], back_r.at[r], nm, m, mates)
+
     for copy in outs:
         copy.wait()
     for copy in sends + mask_copies + halo_copies[0] + halo_copies[1]:
         copy.wait_send()
-
-
-def factor_kernel(n, mb, cells, g_ref, filt_ref, w_ref, out_ref, sem):
-    rows = filt_ref.shape[0]
-    outs = [pltpu.make_async_copy(filt_ref.at[r], out_ref.at[:, r, :], sem.at[r]) for r in range(rows)]
-    for copy in outs:
-        copy.start()
-    nb = 2 * n // mb
-    zeros = jnp.zeros((n, n), jnp.float32)
-    top = g_ref[0].reshape(n, 2 * n)
-    panel = g_ref[1].reshape(n, 2 * n)
-    cross = top[:, n:]
-    full = jnp.concatenate(
-        [top, jnp.concatenate([cross.T, panel[:, :n]], axis=1)], axis=0
-    )
-    w_ref[...] = eliminate(full, n, mb, nb, cells)
-    for copy in outs:
-        copy.wait()
 
 
 def eliminate(full, n, mb, nb, cells):
@@ -337,39 +380,15 @@
     return jnp.concatenate(result, axis=0)
 
 
-def apply_kernel(nm, x_ref, w_ref, out_ref, mixed, send, recv):
-    slab = lax.axis_index("slab")
-    m = lax.axis_index("mode")
-    rows, mb, cols = out_ref.shape
-    wide = cols // nm
-    barrier = pltpu.get_barrier_semaphore()
-    for j in range(1, nm):
-        pl.semaphore_signal(
-            barrier, inc=1, device_id=at(slab, lax.rem(m + j, nm)), device_id_type=pl.DeviceIdType.MESH
-        )
-    pl.semaphore_wait(barrier, nm - 1)
-
-    def columns(peer):
-        return pl.ds(pl.multiple_of(peer * wide, wide), wide)
-
-    def eight(peer):
-        return pl.ds(pl.multiple_of(peer * mb, mb), mb)
-
-    def mates(peer):
-        return at(slab, peer)
-
-    src = lambda r: (lambda peer: mixed.at[r, eight(peer), :])
-    dst = lambda r: (lambda who: out_ref.at[r, :, columns(who)])
-    w = w_ref[...]
-    sends = []
-    for r in range(rows):
-        mixed[r] = jnp.dot(w, x_ref[r], precision=HIGHEST, preferred_element_type=jnp.float32)
-        sends += exchange(src(r), dst(r), send.at[r], recv.at[r], nm, m, mates)
-        out_ref[r, :, columns(m)] = mixed[r, eight(m), :]
-    for r in range(rows):
-        arrive(src(r), dst(r), send.at[r], recv.at[r], nm, m, mates)
-    for copy in sends:
-        copy.wait_send()
+def place_kernel(filt_ref, spread_ref, filtered_ref, orthonormal_ref, sem):
+    copies = []
+    for r in range(filt_ref.shape[0]):
+        copies.append(pltpu.make_async_copy(filt_ref.at[r], filtered_ref.at[:, r, :], sem.at[0, r]))
+        copies.append(pltpu.make_async_copy(spread_ref.at[r], orthonormal_ref.at[:, r, :], sem.at[1, r]))
+    for copy in copies:
+        copy.start()
+    for copy in copies:
+        copy.wait()
 
 
 def shards(ns, nm, block_input, drum_mask, panel):
@@ -379,22 +398,17 @@
     wide = cols // nm
     n = nm * mb
     f32 = jnp.float32
-    pairs = filter_coefficients()
-    coef = jnp.array(
-        [[0.0] + [-first for first, _ in pairs], [0.0] + [second for _, second in pairs]], f32
-    )
     vmem = pl.BlockSpec(memory_space=pltpu.VMEM)
     hbm = pl.BlockSpec(memory_space=pl.ANY)
     dma = pltpu.SemaphoreType.DMA
-    filt, x, g = pl.pallas_call(
-        functools.partial(gather_kernel, nz, ny, nm),
+    filt, spread = pl.pallas_call(
+        functools.partial(whole_kernel, nz, ny, nm, float(ns * rows * cols)),
         out_shape=(
             jax.ShapeDtypeStruct((rows, mb, cols), f32),
-            jax.ShapeDtypeStruct((rows, 2 * n, wide), f32),
-            jax.ShapeDtypeStruct((2, nm, mb, 2 * n), f32),
+            jax.ShapeDtypeStruct((rows, mb, cols), f32),
         ),
-        in_specs=[pl.BlockSpec(memory_space=pltpu.SMEM), hbm, hbm, hbm],
-        out_specs=(hbm, vmem, vmem),
+        in_specs=[hbm, hbm, hbm],
+        out_specs=(hbm, vmem),
         scratch_shapes=[
             pltpu.VMEM((rows, mb, cols), f32),
             pltpu.VMEM((2, rows, mb, cols), f32),
@@ -403,6 +417,8 @@
             pltpu.VMEM((rows, mb, cols), f32),
             pltpu.VMEM((DEGREE + 1, 3 * rows, mb, cols + PAD), f32),
             pltpu.VMEM((3 * rows, mb, cols + PAD), f32),
+            pltpu.VMEM((rows, 2 * n, wide), f32),
+            pltpu.VMEM((rows, 4 * n, wide), jnp.bfloat16),
             pltpu.VMEM((2, nm, mb, 2 * n), f32),
             pltpu.VMEM((2, nm, mb, 2 * n), f32),
             pltpu.VMEM((2, mb, 2 * n), f32),
@@ -410,6 +426,8 @@
             pltpu.VMEM((2, mb, 2 * n), f32),
             pltpu.VMEM((2, nz, mb, 2 * n), f32),
             pltpu.VMEM((2, mb, 2 * n), f32),
+            pltpu.VMEM((2, nm, mb, 2 * n), f32),
+            pltpu.VMEM((rows, n, wide), f32),
             dma((2 * rows + 1,)),
             dma((2, rows)), dma((2, rows)),
             dma((2,)), dma((2,)),
@@ -419,35 +437,24 @@
             dma((2, ny)), dma((2, ny)),
             dma((2, nz)), dma((2, nz)),
             dma((2, nm)), dma((2, nm)),
+            dma((rows, nm)), dma((rows, nm)),
             dma((rows,)),
         ],
-        compiler_params=pltpu.CompilerParams(collective_id=0, has_side_effects=True),
-        name="filter_gram",
-    )(coef, block_input, drum_mask, panel)
-    w, filtered = pl.pallas_call(
-        functools.partial(factor_kernel, n, mb, float(ns * rows * cols)),
-        out_shape=(
-            jax.ShapeDtypeStruct((n, 2 * n), f32),
-            jax.ShapeDtypeStruct((mb, rows, cols), f32),
+        compiler_params=pltpu.CompilerParams(
+            collective_id=0, has_side_effects=True, vmem_limit_bytes=VMEM_LIMIT
         ),
-        in_specs=[vmem, hbm],
-        out_specs=(vmem, hbm),
-        scratch_shapes=[dma((rows,))],
-        name="factor",
-    )(g, filt)
-    spread = pl.pallas_call(
-        functools.partial(apply_kernel, nm),
-        out_shape=jax.ShapeDtypeStruct((rows, mb, cols), f32),
+        name="whole",
+    )(block_input, drum_mask, panel)
+    shape = jax.ShapeDtypeStruct((mb, rows, cols), f32)
+    return pl.pallas_call(
+        place_kernel,
+        out_shape=(shape, shape),
         in_specs=[vmem, vmem],
-        out_specs=vmem,
-        scratch_shapes=[
-            pltpu.VMEM((rows, n, wide), f32),
-            dma((rows, nm)), dma((rows, nm)),
-        ],
-        compiler_params=pltpu.CompilerParams(collective_id=1, has_side_effects=True),
-        name="apply",
-    )(x, w)
-    return (filtered, jnp.transpose(spread, (1, 0, 2)))
+        out_specs=(hbm, hbm),
+        scratch_shapes=[dma((2, rows))],
+        compiler_params=pltpu.CompilerParams(vmem_limit_bytes=8 << 20),
+        name="place",
+    )(filt, spread)
 
 
 def solution(mesh):

time: 94.7 us -> 78.1 us (0.82)
  Pallas kernels: 91.6 us -> 76.4 us
  local copies, waits for them, and re-layouts: 2.14 us -> 0.83 us
    pallas_call x3 -> x2, Pallas kernels: 91.6 us -> 76.4 us  [the longest x1 75.3 us: shards(): pl.pallas_call(functools.partial(whole_kernel, nz, ny, nm, float(ns * row...]
    unnamed x1 -> x2, local copies, waits for them, and re-layouts: 2.14 us -> 0.83 us
where the time goes in v2:
time: 78.1 us; the launch traced here: 77.8 us
  Pallas kernels  76.4 us (98%)
  local copies, waits for them, and re-layouts  0.83 us (1%)
    pallas_call x1, Pallas kernels, shards(): pl.pallas_call(functools.partial(whole_kernel, nz, ny, nm, float(ns * row...  75.3 us

profile of v2, /device:TPU:1, one launch (start us, length us, event | category | flops | bytes accessed | tf_op | source)
XLA Modules:
  0.0 77.8 jit_solution(11470023435827734799)
XLA Ops:
  0.6 0.0 copy-start
  0.6 0.8 %copy-done = s32[8,2048]{1,0:T(8,128)S(1)} copy-done((s32[8,2048]{1,0:T(8,128)S(1)}, s32[8,2048]{1,0:T(8,128)}, u32[]{:S(2)}) %copy-start) | copy-done | bytes 65560
  1.5 75.3 %whole.1 = (f32[8,8,2048]{2,1,0:T(8,128)S(1)}, f32[8,8,2048]{2,1,0:T(8,128)S(1)}) custom-call(f32[8,8,2048]{2,1,0:T(8,128)} %block_ref.1, s32[8,2048]{1,0:T(8,128)S(1)} %copy-done, f32[8,8,2048]{2,1,0:T(8,128)} %panel_ref.1), custom_call_target="tpu_custom_call" | custom-call | tf_op jit(solution)/shard_map/whole/pallas_call | solution.py:404
  76.7 1.1 %place.1 = (f32[8,8,2048]{2,1,0:T(8,128)}, f32[8,8,2048]{2,1,0:T(8,128)}) custom-call(f32[8,8,2048]{2,1,0:T(8,128)S(1)} %get-tuple-element.4.filt_ref, f32[8,8,2048]{2,1,0:T(8,128)S(1)} %get-tuple-element.5.spread_ref), custom_call_target="tpu_custom_call" | custom-call | tf_op jit(solution)/shard_map/place/pallas_call | solution.py:449
Async XLA Ops:
  0.6 0.8 %copy-start = (s32[8,2048]{1,0:T(8,128)S(1)}, s32[8,2048]{1,0:T(8,128)}, u32[]{:S(2)}) copy-start(s32[8,2048]{1,0:T(8,128)} %mask_ref.1) | copy-start | bytes 196612

commit v3 on v2

--- a/solution.py
+++ b/solution.py
@@ -61,13 +61,6 @@
         remote(src(peer), dst(peer), send.at[peer], recv.at[peer], place(peer)).wait_recv()
 
 
-def pick(k, values):
-    out = jnp.float32(values[0])
-    for index in range(1, len(values)):
-        out = jnp.where(k == index, jnp.float32(values[index]), out)
-    return out
-
-
 def halves(value):
     high = value.astype(jnp.bfloat16)
     return high, (value - high.astype(jnp.float32)).astype(jnp.bfloat16)
@@ -76,8 +69,8 @@
 def whole_kernel(
     nz, ny, nm, cells, block_ref, mask_ref, panel_ref,
     filt_ref, spread_ref,
-    raw, halo, mraw, mhalo, pt, y, mf, x, xs, part, rs, tmp, yb, tmpz, zb, tmpg, g, mixed,
-    loc_sem, halo_s, halo_r, mask_s, mask_r, p_s, p_r, z_s, z_r, rs_s, rs_r, y_s, y_r, zz_s, zz_r, ag_s, ag_r,
+    raw, halo, mraw, mhalo, pt, y0, y1, y2, y3, y4, y5, y6, y7, y8, mf, x, xs, part, rs, tmp, yb, tmpz, zb, tmpg, g, mixed,
+    loc_sem, halo_s, halo_r, mask_s, mask_r, pass_s, pass_r, p_s, p_r, z_s, z_r, rs_s, rs_r, y_s, y_r, zz_s, zz_r, ag_s, ag_r,
     back_s, back_r, out_sem,
 ):
     ns = nz * ny
@@ -90,9 +83,13 @@
     n = nm * mb
     up = lax.rem(slab + ns - 1, ns)
     down = lax.rem(slab + 1, ns)
+    y = [y0, y1, y2, y3, y4, y5, y6, y7, y8]
     pairs = filter_coefficients()
-    gain = [0.0] + [-first for first, _ in pairs]
-    drag = [0.0] + [second for _, second in pairs]
+    scale = [1.0]
+    for first, _ in pairs:
+        scale.append(-first * scale[-1])
+    drag = [0.0, 0.0] + [pairs[k - 1][1] * scale[k - 2] / scale[k] for k in range(2, DEGREE + 1)]
+    last = DEGREE
 
     local = [pltpu.make_async_copy(mask_ref, mraw, loc_sem.at[2 * rows])]
     local += [pltpu.make_async_copy(block_ref.at[:, r, :], raw.at[r], loc_sem.at[r]) for r in range(rows)]
@@ -118,9 +115,21 @@
     pl.semaphore_wait(barrier, 2 + nm - 1 + ny - 1 + nz - 1)
 
     sends = []
+    core = lax.rem(m, 2)
+    other = m + 1 - 2 * core
+    half = pl.ds(pl.multiple_of(core * (cols // 2), 128), cols // 2)
+    rest = pl.ds(pl.multiple_of((1 - core) * (cols // 2), 128), cols // 2)
     mask_copies = [
-        remote(mraw, mhalo.at[0], mask_s.at[0], mask_r.at[0], at(down, m)),
-        remote(mraw, mhalo.at[1], mask_s.at[1], mask_r.at[1], at(up, m)),
+        remote(mraw.at[:, half], mhalo.at[0, :, half], mask_s.at[0], mask_r.at[0], at(down, m)),
+        remote(mraw.at[:, half], mhalo.at[1, :, half], mask_s.at[1], mask_r.at[1], at(up, m)),
+    ]
+    mask_passes = [
+        remote(mhalo.at[side, :, half], mhalo.at[side, :, half], pass_s.at[side], pass_r.at[side], at(slab, other))
+        for side in range(2)
+    ]
+    mask_lands = [
+        remote(mhalo.at[side, :, rest], mhalo.at[side, :, rest], pass_s.at[side], pass_r.at[side], at(slab, other))
+        for side in range(2)
     ]
     for copy in mask_copies:
         copy.start()
@@ -161,34 +170,31 @@
         row = jnp.broadcast_to(mraw[r:r + 1, :].astype(jnp.float32), (mb, cols))
         mf[rows + r, :, :cols] = row
         mf[rows + r, :, cols:] = zero_pad
-        y[0, rows + r, :, :cols] = raw[r] * row
-        y[0, rows + r, :, cols:] = zero_pad
+        y0[rows + r, :, :cols] = raw[r] * row
+        y0[rows + r, :, cols:] = zero_pad
 
     def row_step(k, r):
-        here = y[k - 1, r]
-        total = here + y[k - 1, r - 1] + y[k - 1, r + 1]
+        here = y[k - 1][r]
+        total = here + y[k - 1][r - 1] + y[k - 1][r + 1]
         total = total + pltpu.roll(here, 1, 1) + pltpu.roll(here, cols + PAD - 1, 1)
-        before = y[jnp.maximum(k - 2, 0), r]
-        y[k, r] = mf[r] * (total * pick(k, gain)) - before * pick(k, drag)
+        new = mf[r] * total
+        if k > 1:
+            new = new - y[k - 2][r] * drag[k]
+        y[k][r] = new * scale[k] if k == last else new
 
     def stage(d):
-        def body(k, carry):
+        for k in range(1, min(last, d + 3) + 1):
             row_step(k, rows - d + k)
             row_step(k, 2 * rows - 1 + d - k)
-            return carry
-
-        lax.fori_loop(1, min(DEGREE, d + 3) + 1, body, 0)
-
-    def inner(k, carry):
-        def one(r, c):
+
+    for k in range(1, rows // 2):
+        for r in range(rows + k, 2 * rows - k):
             row_step(k, r)
-            return c
-
-        return lax.fori_loop(rows + k, 2 * rows - k, one, carry)
-
-    lax.fori_loop(1, rows // 2, inner, 0)
-
-    for copy in mask_copies:
+
+    for side in range(2):
+        mask_copies[side].wait_recv()
+        mask_passes[side].start()
+    for copy in mask_lands:
         copy.wait_recv()
     inside = [jnp.where(slab > 0, 1.0, 0.0), jnp.where(slab < ns - 1, 1.0, 0.0)]
     for side in range(2):
@@ -198,7 +204,7 @@
             mf[index, :, :cols] = jnp.broadcast_to(row, (mb, cols))
             mf[index, :, cols:] = zero_pad
 
-    z_src = lambda r: (lambda peer: y.at[DEGREE, rows + r, :, columns(peer)])
+    z_src = lambda r: (lambda peer: y8.at[rows + r, :, columns(peer)])
     z_dst = lambda r: (lambda who: x.at[r, eight(who), :])
     contract = (((1,), (1,)), ((), ()))
 
@@ -242,14 +248,14 @@
         for side, r in ((0, rows - d), (1, d - 1)):
             halo_copies[side][d - 1].wait_recv()
             index = r if side == 0 else 2 * rows + r
-            y[0, index, :, :cols] = halo[side, r] * mf[index, :, :cols]
-            y[0, index, :, cols:] = zero_pad
+            y0[index, :, :cols] = halo[side, r] * mf[index, :, :cols]
+            y0[index, :, cols:] = zero_pad
         stage(d)
         if d > rows // 2:
             for r in (rows - d, d - 1):
                 sends += exchange(z_src(r), z_dst(r), z_s.at[r], z_r.at[r], nm, m, mates)
-                x[r, eight(m), :] = y[DEGREE, rows + r, :, columns(m)]
-                out = pltpu.make_async_copy(y.at[DEGREE, rows + r, :, pl.ds(0, cols)], filt_ref.at[r], out_sem.at[r])
+                x[r, eight(m), :] = y8[rows + r, :, columns(m)]
+                out = pltpu.make_async_copy(y8.at[rows + r, :, pl.ds(0, cols)], filt_ref.at[r], out_sem.at[r])
                 out.start()
                 outs.append(out)
         if d in panel_rows:
@@ -329,7 +335,7 @@
 
     for copy in outs:
         copy.wait()
-    for copy in sends + mask_copies + halo_copies[0] + halo_copies[1]:
+    for copy in sends + mask_copies + mask_passes + halo_copies[0] + halo_copies[1]:
         copy.wait_send()
 
 
@@ -415,7 +421,7 @@
             pltpu.VMEM((rows, cols), jnp.int32),
             pltpu.VMEM((2, rows, cols), jnp.int32),
             pltpu.VMEM((rows, mb, cols), f32),
-            pltpu.VMEM((DEGREE + 1, 3 * rows, mb, cols + PAD), f32),
+            *[pltpu.VMEM((3 * rows, mb, cols + PAD), f32)] * (DEGREE + 1),
             pltpu.VMEM((3 * rows, mb, cols + PAD), f32),
             pltpu.VMEM((rows, 2 * n, wide), f32),
             pltpu.VMEM((rows, 4 * n, wide), jnp.bfloat16),
@@ -430,6 +436,7 @@
             pltpu.VMEM((rows, n, wide), f32),
             dma((2 * rows + 1,)),
             dma((2, rows)), dma((2, rows)),
+            dma((2,)), dma((2,)),
             dma((2,)), dma((2,)),
             dma((nm,)), dma((nm,)),
             dma((rows, nm)), dma((rows, nm)),

time: 78.1 us -> 73.8 us (0.945)
  Pallas kernels: 76.4 us -> 72.1 us
    pallas_call x1, Pallas kernels: 75.3 us -> 71 us  [shards(): pl.pallas_call(functools.partial(whole_kernel, nz, ny, nm, float(ns * row...]
where the time goes in v3:
time: 73.8 us; the launch traced here: 73.6 us
  Pallas kernels  72.1 us (98%)
  local copies, waits for them, and re-layouts  0.83 us (1%)
    pallas_call x1, Pallas kernels, shards(): pl.pallas_call(functools.partial(whole_kernel, nz, ny, nm, float(ns * row...  71 us

profile of v3, /device:TPU:1, one launch (start us, length us, event | category | flops | bytes accessed | tf_op | source)
XLA Modules:
  0.0 73.6 jit_solution(12894480901930833304)
XLA Ops:
  0.6 0.0 copy-start
  0.6 0.8 %copy-done = s32[8,2048]{1,0:T(8,128)S(1)} copy-done((s32[8,2048]{1,0:T(8,128)S(1)}, s32[8,2048]{1,0:T(8,128)}, u32[]{:S(2)}) %copy-start) | copy-done | bytes 65560
  1.5 71.0 %whole.1 = (f32[8,8,2048]{2,1,0:T(8,128)S(1)}, f32[8,8,2048]{2,1,0:T(8,128)S(1)}) custom-call(f32[8,8,2048]{2,1,0:T(8,128)} %block_ref.1, s32[8,2048]{1,0:T(8,128)S(1)} %copy-done, f32[8,8,2048]{2,1,0:T(8,128)} %panel_ref.1), custom_call_target="tpu_custom_call" | custom-call | tf_op jit(solution)/shard_map/whole/pallas_call | solution.py:410
  72.5 1.1 %place.1 = (f32[8,8,2048]{2,1,0:T(8,128)}, f32[8,8,2048]{2,1,0:T(8,128)}) custom-call(f32[8,8,2048]{2,1,0:T(8,128)S(1)} %get-tuple-element.4.filt_ref, f32[8,8,2048]{2,1,0:T(8,128)S(1)} %get-tuple-element.5.spread_ref), custom_call_target="tpu_custom_call" | custom-call | tf_op jit(solution)/shard_map/place/pallas_call | solution.py:456
Async XLA Ops:
  0.6 0.8 %copy-start = (s32[8,2048]{1,0:T(8,128)S(1)}, s32[8,2048]{1,0:T(8,128)}, u32[]{:S(2)}) copy-start(s32[8,2048]{1,0:T(8,128)} %mask_ref.1) | copy-start | bytes 196612

commit v4 on v3

--- a/solution.py
+++ b/solution.py
@@ -93,7 +93,7 @@
 
     local = [pltpu.make_async_copy(mask_ref, mraw, loc_sem.at[2 * rows])]
     local += [pltpu.make_async_copy(block_ref.at[:, r, :], raw.at[r], loc_sem.at[r]) for r in range(rows)]
-    local += [pltpu.make_async_copy(panel_ref.at[:, r, :], pt.at[r], loc_sem.at[rows + r]) for r in range(rows)]
+    late = [pltpu.make_async_copy(panel_ref.at[:, r, :], pt.at[r], loc_sem.at[rows + r]) for r in range(rows)]
     for copy in local:
         copy.start()
 
@@ -110,8 +110,7 @@
         greet(at(zi * ny + lax.rem(yi + j, ny), m))
     for j in range(1, nz):
         greet(at(lax.rem(zi + j, nz) * ny + yi, m))
-    for copy in local[: 1 + rows]:
-        copy.wait()
+    local[0].wait()
     pl.semaphore_wait(barrier, 2 + nm - 1 + ny - 1 + nz - 1)
 
     sends = []
@@ -136,13 +135,18 @@
     halo_copies = [[], []]
     for d in range(1, rows + 1):
         lo, hi = rows - d, d - 1
+        if lo > hi:
+            local[1 + lo].wait()
+            local[1 + hi].wait()
         top = remote(raw.at[lo], halo.at[0, lo], halo_s.at[0, lo], halo_r.at[0, lo], at(down, m))
         bottom = remote(raw.at[hi], halo.at[1, hi], halo_s.at[1, hi], halo_r.at[1, hi], at(up, m))
         top.start()
         bottom.start()
         halo_copies[0].append(top)
         halo_copies[1].append(bottom)
-    for copy in local[1 + rows:]:
+    for copy in late:
+        copy.start()
+    for copy in late:
         copy.wait()
 
     def mates(peer):
@@ -350,7 +354,8 @@
         inside = (lane >= base) & (lane < base + mb)
         block = a[b]
         rowb = [jnp.broadcast_to(block[i:i + 1, :], (mb, width)) for i in range(mb)]
-        e = [[jnp.broadcast_to(rowb[i][:, base + j:base + j + 1], (mb, width)) for j in range(i + 1)] for i in range(mb)]
+        own = [jnp.broadcast_to(block[:, base + k:base + k + 1], (mb, width)) for k in range(mb)]
+        e = [[jnp.broadcast_to(own[j][i:i + 1, :], (mb, width)) for j in range(i + 1)] for i in range(mb)]
         later = range(b + 1, nb)
         column = {
             i: [jnp.broadcast_to(a[i][:, base + k:base + k + 1], (mb, width)) for k in range(mb)] for i in later
@@ -358,15 +363,19 @@
         row = [jnp.where(inside, jnp.where(lane == base + i, 1.0, 0.0), rowb[i]) for i in range(mb)]
         pivot, inverse = [], []
         f = [[None] * mb for _ in range(mb)]
-        for k in range(mb):
-            pivot.append(e[k][k])
-            inverse.append(1.0 / e[k][k])
-            for i in range(k + 1, mb):
-                f[i][k] = e[i][k] * inverse[k]
-            for i in range(k + 1, mb):
-                for j in range(k + 1, i + 1):
-                    e[i][j] = e[i][j] - f[i][k] * e[j][k]
-                row[i] = row[i] - f[i][k] * row[k]
+        for k in range(0, mb, 2):
+            first, link = e[k][k], e[k + 1][k]
+            det = first * e[k + 1][k + 1] - link * link
+            first_inverse = 1.0 / first
+            pivot += [first, det * first_inverse]
+            inverse += [first_inverse, first * (1.0 / det)]
+            for step in (k, k + 1):
+                for i in range(step + 1, mb):
+                    f[i][step] = e[i][step] * inverse[step]
+                for i in range(step + 1, mb):
+                    for j in range(step + 1, i + 1):
+                        e[i][j] = e[i][j] - f[i][step] * e[j][step]
+                    row[i] = row[i] - f[i][step] * row[step]
         if base >= n:
             scaled = jnp.zeros((mb, width), jnp.float32)
             for i in range(mb):

time: 73.8 us -> 73.4 us (level)
  no operation moved by 1% of the time
where the time goes in v4:
time: 73.4 us; the launch traced here: 73.2 us
  Pallas kernels  71.7 us (98%)
  local copies, waits for them, and re-layouts  0.83 us (1%)
    pallas_call x1, Pallas kernels, shards(): pl.pallas_call(functools.partial(whole_kernel, nz, ny, nm, float(ns * row...  70.6 us

profile of v4, /device:TPU:1, one launch (start us, length us, event | category | flops | bytes accessed | tf_op | source)
XLA Modules:
  0.0 73.2 jit_solution(5625190980278346305)
XLA Ops:
  0.6 0.0 copy-start
  0.6 0.8 %copy-done = s32[8,2048]{1,0:T(8,128)S(1)} copy-done((s32[8,2048]{1,0:T(8,128)S(1)}, s32[8,2048]{1,0:T(8,128)}, u32[]{:S(2)}) %copy-start) | copy-done | bytes 65560
  1.5 70.6 %whole.1 = (f32[8,8,2048]{2,1,0:T(8,128)S(1)}, f32[8,8,2048]{2,1,0:T(8,128)S(1)}) custom-call(f32[8,8,2048]{2,1,0:T(8,128)} %block_ref.1, s32[8,2048]{1,0:T(8,128)S(1)} %copy-done, f32[8,8,2048]{2,1,0:T(8,128)} %panel_ref.1), custom_call_target="tpu_custom_call" | custom-call | tf_op jit(solution)/shard_map/whole/pallas_call | solution.py:419
  72.1 1.1 %place.1 = (f32[8,8,2048]{2,1,0:T(8,128)}, f32[8,8,2048]{2,1,0:T(8,128)}) custom-call(f32[8,8,2048]{2,1,0:T(8,128)S(1)} %get-tuple-element.4.filt_ref, f32[8,8,2048]{2,1,0:T(8,128)S(1)} %get-tuple-element.5.spread_ref), custom_call_target="tpu_custom_call" | custom-call | tf_op jit(solution)/shard_map/place/pallas_call | solution.py:465
Async XLA Ops:
  0.6 0.8 %copy-start = (s32[8,2048]{1,0:T(8,128)S(1)}, s32[8,2048]{1,0:T(8,128)}, u32[]{:S(2)}) copy-start(s32[8,2048]{1,0:T(8,128)} %mask_ref.1) | copy-start | bytes 196612

commit v5 on v4

--- a/solution.py
+++ b/solution.py
@@ -71,7 +71,7 @@
     filt_ref, spread_ref,
     raw, halo, mraw, mhalo, pt, y0, y1, y2, y3, y4, y5, y6, y7, y8, mf, x, xs, part, rs, tmp, yb, tmpz, zb, tmpg, g, mixed,
     loc_sem, halo_s, halo_r, mask_s, mask_r, pass_s, pass_r, p_s, p_r, z_s, z_r, rs_s, rs_r, y_s, y_r, zz_s, zz_r, ag_s, ag_r,
-    back_s, back_r, out_sem,
+    back_s, back_r, out_sem, known,
 ):
     ns = nz * ny
     slab = lax.axis_index("slab")
@@ -106,12 +106,24 @@
     greet(at(down, m))
     for j in range(1, nm):
         greet(at(slab, lax.rem(m + j, nm)))
-    for j in range(1, ny):
-        greet(at(zi * ny + lax.rem(yi + j, ny), m))
-    for j in range(1, nz):
-        greet(at(lax.rem(zi + j, nz) * ny + yi, m))
+    def near(step):
+        return [
+            at(zi * ny + lax.rem(yi + step, ny), m),
+            at(zi * ny + lax.rem(yi + ny - step, ny), m),
+            at(lax.rem(zi + step, nz) * ny + yi, m),
+            at(lax.rem(zi + nz - step, nz) * ny + yi, m),
+        ]
+
+    def tell(index, step):
+        for where in near(step):
+            pl.semaphore_signal(
+                known.at[index], inc=1, device_id=where, device_id_type=pl.DeviceIdType.MESH
+            )
+
+    for where in near(1):
+        greet(where)
     local[0].wait()
-    pl.semaphore_wait(barrier, 2 + nm - 1 + ny - 1 + nz - 1)
+    pl.semaphore_wait(barrier, 2 + nm - 1 + 4)
 
     sends = []
     core = lax.rem(m, 2)
@@ -146,6 +158,7 @@
         halo_copies[1].append(bottom)
     for copy in late:
         copy.start()
+    tell(0, 1)
     for copy in late:
         copy.wait()
 
@@ -195,6 +208,8 @@
         for r in range(rows + k, 2 * rows - k):
             row_step(k, r)
 
+    pl.semaphore_wait(known.at[0], 4)
+    tell(1, 2)
     for side in range(2):
         mask_copies[side].wait_recv()
         mask_passes[side].start()
@@ -270,6 +285,7 @@
                 panel_part += same
                 panel_mixed += cross
         if d == rows - 2:
+            pl.semaphore_wait(known.at[1], 4)
             panel_all = panel_part + panel_mixed + panel_mixed.T
             panel_all = jnp.concatenate([panel_all, jnp.zeros((n, n), jnp.float32)], axis=1)
             for j in range(nm):
@@ -455,6 +471,7 @@
             dma((2, nm)), dma((2, nm)),
             dma((rows, nm)), dma((rows, nm)),
             dma((rows,)),
+            pltpu.SemaphoreType.REGULAR((2,)),
         ],
         compiler_params=pltpu.CompilerParams(
             collective_id=0, has_side_effects=True, vmem_limit_bytes=VMEM_LIMIT

time: 73.4 us -> 72.6 us (0.989)
  Pallas kernels: 71.7 us -> 70.9 us
    pallas_call x1, Pallas kernels: 70.6 us -> 69.8 us  [shards(): pl.pallas_call(functools.partial(whole_kernel, nz, ny, nm, float(ns * row...]
where the time goes in v5:
time: 72.6 us; the launch traced here: 72.4 us
  Pallas kernels  70.9 us (98%)
  local copies, waits for them, and re-layouts  0.83 us (1%)
    pallas_call x1, Pallas kernels, shards(): pl.pallas_call(functools.partial(whole_kernel, nz, ny, nm, float(ns * row...  69.8 us

profile of v5, /device:TPU:1, one launch (start us, length us, event | category | flops | bytes accessed | tf_op | source)
XLA Modules:
  0.0 72.4 jit_solution(459944791925048410)
XLA Ops:
  0.6 0.0 copy-start
  0.6 0.8 %copy-done = s32[8,2048]{1,0:T(8,128)S(1)} copy-done((s32[8,2048]{1,0:T(8,128)S(1)}, s32[8,2048]{1,0:T(8,128)}, u32[]{:S(2)}) %copy-start) | copy-done | bytes 65560
  1.5 69.8 %whole.1 = (f32[8,8,2048]{2,1,0:T(8,128)S(1)}, f32[8,8,2048]{2,1,0:T(8,128)S(1)}) custom-call(f32[8,8,2048]{2,1,0:T(8,128)} %block_ref.1, s32[8,2048]{1,0:T(8,128)S(1)} %copy-done, f32[8,8,2048]{2,1,0:T(8,128)} %panel_ref.1), custom_call_target="tpu_custom_call" | custom-call | tf_op jit(solution)/shard_map/whole/pallas_call | solution.py:435
  71.3 1.1 %place.1 = (f32[8,8,2048]{2,1,0:T(8,128)}, f32[8,8,2048]{2,1,0:T(8,128)}) custom-call(f32[8,8,2048]{2,1,0:T(8,128)S(1)} %get-tuple-element.4.filt_ref, f32[8,8,2048]{2,1,0:T(8,128)S(1)} %get-tuple-element.5.spread_ref), custom_call_target="tpu_custom_call" | custom-call | tf_op jit(solution)/shard_map/place/pallas_call | solution.py:482
Async XLA Ops:
  0.6 0.8 %copy-start = (s32[8,2048]{1,0:T(8,128)S(1)}, s32[8,2048]{1,0:T(8,128)}, u32[]{:S(2)}) copy-start(s32[8,2048]{1,0:T(8,128)} %mask_ref.1) | copy-start | bytes 196612
